TPU v7x, 256 devices: a whole 4x4x8 slice. The times are simulated.
256 devices in a mesh: lat: 32 (over x, z), lead: 8 (over y, core).
Axes of the slice: x: 4, y: 4, z: 8, core: 2. Of those that a mesh axis runs over, the one named last changes fastest.
Arguments:
- latent: bfloat16 [32, 256, 64, 256], P('lat', None, 'lead'), may hold values from -6 to 6
- conv_weight: bfloat16 [3, 3, 256, 256], replicated, may hold values from -0.125 to 0.125
- conv_bias: float32 [256], replicated, may hold values from -4 to 4
- norm_gain: float32 [256], replicated, may hold values from 0.1 to 1.9
- w_query: bfloat16 [256, 256], replicated, may hold values from -12 to 12
- w_key: bfloat16 [256, 256], replicated, may hold values from -0.25 to 0.25
- w_value: bfloat16 [256, 256], replicated, may hold values from -0.375 to 0.375
- w_out: bfloat16 [256, 256], replicated, may hold values from -0.375 to 0.375
Outputs:
- section_out: bfloat16 [32, 256, 64, 256], P('lat', None, 'lead')
All inputs are finite; a program needn't handle non-finite values.
Results may differ from a plain program's by a relative error of at most 0.014.
Values may be sent and summed in bfloat16 or wider, within the bound.
No kernel may reach another device: no remote copies, remote signals or barrier semaphores. Data moves between devices by JAX's collectives and lax.ppermute only.
A program may use at most 128 MiB of HBM per device.

v0:
```python
import math
import jax
import jax.numpy as jnp
from jax import lax
from jax.sharding import PartitionSpec as P

HD = 32


def padded_2(block, sides, width):
    for axis, dim in sides:
        count = lax.axis_size(axis)
        forward = [(i, i + 1) for i in range(count - 1)]
        backward = [(target, source) for source, target in forward]
        low = lax.ppermute(
            lax.slice_in_dim(block, block.shape[dim] - width, None, axis=dim), axis, forward
        )
        high = lax.ppermute(lax.slice_in_dim(block, 0, width, axis=dim), axis, backward)
        block = jnp.concatenate([low, block, high], axis=dim)
    return block


def attend(query, keys, values):
    chans = query.shape[-1]
    heads = chans // HD
    q_shape = query.shape
    query = query.reshape(-1, q_shape[-2], heads, HD)
    keys = keys.reshape(-1, keys.shape[-2], heads, HD)
    values = values.reshape(-1, values.shape[-2], heads, HD)
    scores = jnp.einsum(
        "pqhd,pkhd->phqk", query, keys, preferred_element_type=jnp.float32
    ) / math.sqrt(HD)
    top = jnp.max(scores, axis=-1, keepdims=True)
    expo = jnp.exp(scores - top)
    weights = (expo / jnp.sum(expo, axis=-1, keepdims=True)).astype(jnp.bfloat16)
    attended = jnp.einsum("phqk,pkhd->pqhd", weights, values, preferred_element_type=jnp.float32)
    return attended.astype(jnp.bfloat16).reshape(q_shape)


def project(normed, weight):
    shape = normed.shape
    flat = jnp.dot(normed.reshape(-1, shape[-1]), weight, preferred_element_type=jnp.float32)
    return flat.astype(jnp.bfloat16).reshape(shape)


def shards(latent, conv_weight, conv_bias, norm_gain, w_query, w_key, w_value, w_out):
    nrows, width, leads, chans = latent.shape
    extended = padded_2(latent, (("lat", 0),), 1)
    padded = jnp.pad(extended, ((0, 0), (1, 1), (0, 0), (0, 0)))
    acc = jnp.zeros((nrows * width * leads, chans), jnp.float32)
    for a in range(3):
        for b in range(3):
            piece = padded[a : a + nrows, b : b + width].reshape(-1, chans)
            acc = acc + jnp.dot(piece, conv_weight[a, b], preferred_element_type=jnp.float32)
    hidden = jax.nn.gelu(acc + conv_bias, approximate=True).astype(jnp.bfloat16)
    hidden_f = hidden.astype(jnp.float32)
    mean = jnp.mean(hidden_f, axis=-1, keepdims=True)
    var = jnp.mean((hidden_f - mean) ** 2, axis=-1, keepdims=True)
    normed = ((hidden_f - mean) * lax.rsqrt(var + 1e-05) * norm_gain).astype(jnp.bfloat16)
    normed = normed.reshape(nrows, width, leads, chans)
    block = lax.all_to_all(normed, "lead", split_axis=1, concat_axis=2, tiled=True)
    attended_px = attend(project(block, w_query), project(block, w_key), project(block, w_value))
    attended = lax.all_to_all(attended_px, "lead", split_axis=2, concat_axis=1, tiled=True)
    mixed = hidden_f + jnp.dot(
        attended.reshape(-1, chans), w_out, preferred_element_type=jnp.float32
    )
    return mixed.astype(jnp.bfloat16).reshape(nrows, width, leads, chans)


def solution(mesh):
    in_specs = (P("lat", None, "lead", None), P(), P(), P(), P(), P(), P(), P())
    out_specs = P("lat", None, "lead", None)
    return jax.shard_map(shards, mesh=mesh, in_specs=in_specs, out_specs=out_specs, check_vma=False)
```

profile of v0, /device:TPU:6, one launch (start us, length us, event | category | flops | bytes accessed | tf_op | source)
XLA Modules:
  0.0 127.0 jit_solution(6796232368115607537)
XLA Ops:
  0.0 8.1 %collective-permute-start.1 = (bf16[1,256,8,256]{3,2,1,0:T(8,128)(2,1)}, bf16[1,256,8,256]{3,2,1,0:T(8,128)(2,1)S(1)}, u32[]{:S(2)}, u32[]{:S(2)}) collective-permute-start(bf16[1,256,8,256]{3,2,1,0:T(8,128)(2,1)} %param.8), channel_id=1, source_target_pairs={{8,0},{16,8},{24,16},{32,24},{40,32},{48,40},{56,48},{64,56},{72,6... | collective-permute-start | bytes 3145736 | tf_op jit(solution)/shard_map/ppermute | solution.py:18
  8.2 1.9 %collective-permute-start = (bf16[1,256,8,256]{3,2,1,0:T(8,128)(2,1)}, bf16[1,256,8,256]{3,2,1,0:T(8,128)(2,1)S(1)}, u32[]{:S(2)}, u32[]{:S(2)}) collective-permute-start(bf16[1,256,8,256]{3,2,1,0:T(8,128)(2,1)} %param.8), channel_id=1, source_target_pairs={{0,8},{8,16},{16,24},{24,32},{32,40},{40,48},{48,56},{56,64},{64,7... | collective-permute-start | bytes 3145736 | tf_op jit(solution)/shard_map/ppermute | solution.py:15
  10.1 1.7 %fusion.46 = f32[2048,256]{1,0:T(8,128)S(1)} fusion(bf16[1,256,8,256]{3,2,1,0:T(8,128)(2,1)} %param.8, bf16[3,3,256,256]{3,2,1,0:T(8,128)(2,1)} %param.9), kind=kOutput, calls=%fused_computation.61 | convolution fusion | flops 268435456 | bytes 3276800 | tf_op jit(solution)/shard_map/dot_general | solution.py:54
  11.8 19.1 %collective-permute-done.1 = bf16[1,256,8,256]{3,2,1,0:T(8,128)(2,1)S(1)} collective-permute-done((bf16[1,256,8,256]{3,2,1,0:T(8,128)(2,1)}, bf16[1,256,8,256]{3,2,1,0:T(8,128)(2,1)S(1)}, u32[]{:S(2)}, u32[]{:S(2)}) %collective-permute-start.1) | collective-permute-done | bytes 1048608 | tf_op jit(solution)/shard_map/ppermute | solution.py:18
  30.9 6.1 %collective-permute-done = bf16[1,256,8,256]{3,2,1,0:T(8,128)(2,1)S(1)} collective-permute-done((bf16[1,256,8,256]{3,2,1,0:T(8,128)(2,1)}, bf16[1,256,8,256]{3,2,1,0:T(8,128)(2,1)S(1)}, u32[]{:S(2)}, u32[]{:S(2)}) %collective-permute-start) | collective-permute-done | bytes 1048608 | tf_op jit(solution)/shard_map/ppermute | solution.py:15
  40.9 1.7 %convert_reduce_fusion = (f32[2048]{0:T(1024)S(1)}, bf16[2048,256]{1,0:T(8,128)(2,1)S(1)}) fusion(f32[256]{0:T(256)S(1)} %copy-done.8, f32[2048,256]{1,0:T(8,128)S(1)} %fusion.39, f32[2048,256]{1,0:T(8,128)S(1)} %fusion.44, f32[2048,256]{1,0:T(8,128)S(1)} %fusion.40, bf16[3,3,256,256]{3,2,1,0:T(8,128)(2,1)S(1)} %copy-done.4, ...), kind=kOutput, calls=%fused_computation.17 | convolution fusion | flops 278919168 | bytes 19014656 | tf_op jit(solution)/shard_map/dot_general | solution.py:54
  42.6 0.6 fusion.19
  43.3 0.7 fusion.38
  44.0 20.4 %all_to_all.30 = bf16[1,256,8,256]{3,2,0,1:T(8,128)(2,1)S(1)} all-to-all(bf16[1,256,8,256]{3,2,0,1:T(8,128)(2,1)S(1)} %fusion.38), channel_id=1, replica_groups=mesh['lat'=32,'lead'=8] {'lead'}, dimensions={1} | all-to-all | bytes 2097152 | tf_op jit(solution)/shard_map/all_to_all | solution.py:61
  64.6 1.4 %convolution_convert_fusion = bf16[2048,256]{1,0:T(8,128)(2,1)} fusion(bf16[2048,256]{1,0:T(8,128)(2,1)S(1)} %bitcast.91, bf16[256,256]{1,0:T(8,128)(2,1)S(1)} %copy-done), kind=kOutput, calls=%fused_computation.25 | convolution fusion | flops 268959744 | bytes 2228224 | tf_op jit(solution)/shard_map/dot_general | solution.py:42
  66.0 1.5 %copy.36 = bf16[2048,256]{0,1:T(8,128)(2,1)S(1)} copy(bf16[2048,256]{1,0:T(8,128)(2,1)} %convolution_convert_fusion) | data formatting | bytes 2097152 | tf_op jit(solution)/shard_map/convert_element_type | solution.py:43
  67.5 3.2 %reshape_reshape.11 = bf16[32,64,8,32]{1,0,3,2:T(8,128)(2,1)} reshape(bf16[2048,256]{0,1:T(8,128)(2,1)S(1)} %copy.36) | data formatting | bytes 2097152 | tf_op jit(solution)/shard_map/reshape;reshape | solution.py:28
  71.1 1.4 %convolution_convert_fusion.2 = bf16[2048,256]{1,0:T(8,128)(2,1)} fusion(bf16[2048,256]{1,0:T(8,128)(2,1)S(1)} %bitcast.93, bf16[256,256]{1,0:T(8,128)(2,1)S(1)} %copy-done.6), kind=kOutput, calls=%fused_computation.27 | convolution fusion | flops 268959744 | bytes 2228224 | tf_op jit(solution)/shard_map/dot_general | solution.py:42
  72.5 2.3 %copy.34 = bf16[2048,256]{0,1:T(8,128)(2,1)} copy(bf16[2048,256]{1,0:T(8,128)(2,1)} %convolution_convert_fusion.2) | data formatting | bytes 2097152 | tf_op jit(solution)/shard_map/convert_element_type | solution.py:43
  74.8 0.6 copy.35
  75.4 3.2 %reshape_reshape.10 = bf16[32,64,8,32]{1,0,3,2:T(8,128)(2,1)} reshape(bf16[2048,256]{0,1:T(8,128)(2,1)S(1)} %copy.35) | data formatting | bytes 2097152 | tf_op jit(solution)/shard_map/reshape;reshape | solution.py:27
  78.6 4.6 %reshape_reshape.9 = bf16[32,64,8,32]{1,0,3,2:T(8,128)(2,1)} reshape(bf16[2048,256]{0,1:T(8,128)(2,1)} %copy.34) | data formatting | bytes 2097152 | tf_op jit(solution)/shard_map/reshape;reshape | solution.py:29
  83.2 4.4 %fusion.31 = f32[32,8,64,64]{2,3,1,0:T(8,128)S(1)} fusion(bf16[32,64,8,32]{1,0,3,2:T(8,128)(2,1)S(1)} %copy-done.1, bf16[32,64,8,32]{1,0,3,2:T(8,128)(2,1)} %reshape_reshape.10), kind=kOutput, calls=%fused_computation.42 | convolution fusion | flops 67108864 | bytes 6291456 | tf_op jit(solution)/shard_map/pqhd,pkhd->phqk/dot_general | solution.py:30
  87.5 12.2 %fusion.69 = (f32[32,8,64]{2,1,0:T(8,128)S(1)}, f32[32,8,64,64]{2,3,1,0:T(8,128)S(1)}) fusion(f32[32,8,64,64]{2,3,1,0:T(8,128)S(1)} %fusion.31), kind=kOutput, calls=%fused_computation.87 | output fusion | flops 4194367 | bytes 8454144 | tf_op jit(solution)/shard_map/sub | solution.py:34
  99.7 3.8 %fusion.34 = bf16[32,8,32,64]{3,2,1,0:T(8,128)(2,1)} fusion(f32[32,8,64,64]{2,3,1,0:T(8,128)S(1)} %get-tuple-element.8, f32[32,8,64]{2,1,0:T(8,128)S(1)} %get-tuple-element.7, bf16[32,64,8,32]{1,0,3,2:T(8,128)(2,1)S(1)} %copy-done.3), kind=kOutput, calls=%fused_computation.45 | convolution fusion | flops 69730304 | bytes 6356992 | tf_op jit(solution)/shard_map/phqk,pkhd->pqhd/dot_general | solution.py:36
  103.5 2.7 %copy.41 = bf16[1,32,64,256]{3,1,0,2:T(8,128)(2,1)S(1)} copy(bf16[1,32,64,256]{2,3,1,0:T(8,128)(2,1)} %bitcast.97) | data formatting | bytes 2097152 | tf_op jit(solution)/shard_map/reshape | solution.py:37
  106.2 18.5 %all_to_all.31 = bf16[1,32,64,256]{3,1,0,2:T(8,128)(2,1)S(1)} all-to-all(bf16[1,32,64,256]{3,1,0,2:T(8,128)(2,1)S(1)} %copy.41), channel_id=1, replica_groups=mesh['lat'=32,'lead'=8] {'lead'}, dimensions={2} | all-to-all | bytes 2097152 | tf_op jit(solution)/shard_map/all_to_all | solution.py:63
  124.7 0.6 copy.54
  125.6 1.4 %fusion.37 = bf16[1,256,8,256]{3,2,1,0:T(8,128)(2,1)} fusion(bf16[2048,256]{1,0:T(8,128)(2,1)S(1)} %bitcast.94, bf16[256,256]{1,0:T(8,128)(2,1)S(1)} %copy-done.7, bf16[2048,256]{1,0:T(8,128)(2,1)S(1)} %get-tuple-element.6), kind=kOutput, calls=%fused_computation.46 | convolution fusion | flops 270008320 | bytes 3276800 | tf_op jit(solution)/shard_map/dot_general | solution.py:64
  (33 shorter events, 4.7 us)
Async XLA Ops:
  0.0 64.5 %copy-start = (bf16[256,256]{1,0:T(8,128)(2,1)S(1)}, bf16[256,256]{1,0:T(8,128)(2,1)}, u32[]{:S(2)}) copy-start(bf16[256,256]{1,0:T(8,128)(2,1)} %param.13) | copy-start | bytes 393220
  0.0 37.0 %copy-start.2 = (bf16[1,256,8,256]{3,2,1,0:T(8,128)(2,1)S(1)}, bf16[1,256,8,256]{3,2,1,0:T(8,128)(2,1)}, u32[]{:S(2)}) copy-start(bf16[1,256,8,256]{3,2,1,0:T(8,128)(2,1)} %param.8) | copy-start | bytes 3145732
  0.0 30.9 %collective-permute-start.1 = (bf16[1,256,8,256]{3,2,1,0:T(8,128)(2,1)}, bf16[1,256,8,256]{3,2,1,0:T(8,128)(2,1)S(1)}, u32[]{:S(2)}, u32[]{:S(2)}) collective-permute-start(bf16[1,256,8,256]{3,2,1,0:T(8,128)(2,1)} %param.8), channel_id=1, source_target_pairs={{8,0},{16,8},{24,16},{32,24},{40,32},{48,40},{56,48},{64,56},{72,6... | collective-permute-start | bytes 3145736 | tf_op jit(solution)/shard_map/ppermute | solution.py:18
  8.2 28.8 %collective-permute-start = (bf16[1,256,8,256]{3,2,1,0:T(8,128)(2,1)}, bf16[1,256,8,256]{3,2,1,0:T(8,128)(2,1)S(1)}, u32[]{:S(2)}, u32[]{:S(2)}) collective-permute-start(bf16[1,256,8,256]{3,2,1,0:T(8,128)(2,1)} %param.8), channel_id=1, source_target_pairs={{0,8},{8,16},{16,24},{24,32},{32,40},{40,48},{48,56},{56,64},{64,7... | collective-permute-start | bytes 3145736 | tf_op jit(solution)/shard_map/ppermute | solution.py:15
  11.8 25.8 %copy-start.4 = (bf16[3,3,256,256]{3,2,1,0:T(8,128)(2,1)S(1)}, bf16[3,3,256,256]{3,2,1,0:T(8,128)(2,1)}, u32[]{:S(2)}) copy-start(bf16[3,3,256,256]{3,2,1,0:T(8,128)(2,1)} %param.9) | copy-start | bytes 3538948
  40.2 0.7 copy-start.8
  40.9 2.4 %copy-start.9 = (f32[256]{0:T(256)S(1)}, f32[256]{0:T(256)}, u32[]{:S(2)}) copy-start(f32[256]{0:T(256)} %param.11) | copy-start | bytes 3076
  67.4 3.2 %copy-start.5 = (bf16[256,256]{1,0:T(8,128)(2,1)S(1)}, bf16[256,256]{1,0:T(8,128)(2,1)}, u32[]{:S(2)}) copy-start(bf16[256,256]{1,0:T(8,128)(2,1)} %param.12) | copy-start | bytes 393220
  67.5 3.7 %copy-start.6 = (bf16[256,256]{1,0:T(8,128)(2,1)S(1)}, bf16[256,256]{1,0:T(8,128)(2,1)}, u32[]{:S(2)}) copy-start(bf16[256,256]{1,0:T(8,128)(2,1)} %param.14) | copy-start | bytes 393220
  78.6 4.6 %copy-start.1 = (bf16[32,64,8,32]{1,0,3,2:T(8,128)(2,1)S(1)}, bf16[32,64,8,32]{1,0,3,2:T(8,128)(2,1)}, u32[]{:S(2)}) copy-start(bf16[32,64,8,32]{1,0,3,2:T(8,128)(2,1)} %reshape_reshape.11) | copy-start | bytes 3145732
  87.5 12.2 %copy-start.3 = (bf16[32,64,8,32]{1,0,3,2:T(8,128)(2,1)S(1)}, bf16[32,64,8,32]{1,0,3,2:T(8,128)(2,1)}, u32[]{:S(2)}) copy-start(bf16[32,64,8,32]{1,0,3,2:T(8,128)(2,1)} %reshape_reshape.9) | copy-start | bytes 3145732
  124.7 0.9 copy-start.7
where the time goes:
time: 127 us
  blocking collectives  38.9 us (31%)
  waiting for transfers between devices  25.2 us (20%)
  local copies, waits for them, and re-layouts  19.3 us (15%)
  matrix products  19.2 us (15%)
  other arithmetic  14.1 us (11%)
  starting transfers between devices  10.1 us (8%)
    all_to_all x1, blocking collectives, shards(): lax.all_to_all(normed, 'lead', split_axis=1, concat_axis=2, tiled=True)  20.4 us
    ppermute x1, waiting for transfers between devices, padded_2(): lax.ppermute(lax.slice_in_dim(block, 0, width, axis=dim), axis, backward)  19.1 us
    all_to_all x1, blocking collectives, shards(): lax.all_to_all(attended_px, 'lead', split_axis=2, concat_axis=1, tiled=True)  18.5 us
    sub x1, other arithmetic, attend(): expo = jnp.exp(scores - top)  12.2 us
    ppermute x1, starting transfers between devices, padded_2(): lax.ppermute(lax.slice_in_dim(block, 0, width, axis=dim), axis, backward)  8.15 us
    dot_general x9, matrix products, shards(): jnp.dot(piece, conv_weight[a, b], preferred_element_type=jnp.float32)  6.44 us
    ppermute x1, waiting for transfers between devices, padded_2(): lax.ppermute(lax.slice_in_dim(block, block.shape[dim] - width, None, axis...  6.12 us
    another operation x1, local copies, waits for them, and re-layouts, attend(): values = values.reshape(-1, values.shape[-2], heads, HD)  4.55 us
  transfers between devices with their start and end apart: 2, of which 2 were waited for; matrix products, arithmetic and copies ran while one was open for 1% of the time, Pallas kernels for 0%

commit v1 on v0

--- a/solution.py
+++ b/solution.py
@@ -1,3 +1,4 @@
+import functools
 import math
 import jax
 import jax.numpy as jnp
@@ -5,6 +6,33 @@
 from jax.sharding import PartitionSpec as P
 
 HD = 32
+
+
+def launch_ports(xx, ax_name):
+    val = lax.axis_size(ax_name)
+    v_next, lower = (val, lax.axis_index(ax_name))
+    a_now = list(xx.shape)
+    val2 = xx.shape[1] // v_next
+    a_now[1] = val2
+    a_next = a_now[2]
+    a_now[2] = a_next * v_next
+    aux = jnp.zeros(a_now, xx.dtype)
+    dev_i = 0
+    while dev_i < v_next:
+        finding = lax.dynamic_slice_in_dim(xx, (lower ^ dev_i) * val2, val2, axis=1)
+        if dev_i:
+            frames = []
+            no = 0
+            while no < v_next:
+                frames.append((no, no ^ dev_i))
+                no += 1
+            finding = lax.ppermute(finding, ax_name, frames)
+        aux = lax.dynamic_update_slice_in_dim(aux, finding, (lower ^ dev_i) * a_next, axis=2)
+        dev_i += 1
+    return aux
+
+
+sector_supply = functools.partial(launch_ports, ax_name="lead")
 
 
 def padded_2(block, sides, width):
@@ -58,7 +86,7 @@
     var = jnp.mean((hidden_f - mean) ** 2, axis=-1, keepdims=True)
     normed = ((hidden_f - mean) * lax.rsqrt(var + 1e-05) * norm_gain).astype(jnp.bfloat16)
     normed = normed.reshape(nrows, width, leads, chans)
-    block = lax.all_to_all(normed, "lead", split_axis=1, concat_axis=2, tiled=True)
+    block = sector_supply(normed)
     attended_px = attend(project(block, w_query), project(block, w_key), project(block, w_value))
     attended = lax.all_to_all(attended_px, "lead", split_axis=2, concat_axis=1, tiled=True)
     mixed = hidden_f + jnp.dot(

time: 127 us -> 119 us (0.937)
  blocking collectives: 38.9 us -> 19.5 us
  starting transfers between devices: 10.1 us -> 18.4 us
  waiting for transfers between devices: 25.2 us -> 32.9 us
  other arithmetic: 14.1 us -> 6.44 us
  matrix products: 19.2 us -> 23.9 us
  local copies, waits for them, and re-layouts: 19.3 us -> 17.3 us
    all_to_all x1 -> x0, blocking collectives: 20.4 us -> none  [shards(): lax.all_to_all(normed, 'lead', split_axis=1, concat_axis=2, tiled=True)]
    ppermute x1, waiting for transfers between devices: 19.1 us -> 1.29 us  [padded_2(): lax.ppermute(lax.slice_in_dim(block, 0, width, axis=dim), axis, backward)]
    ppermute x1, waiting for transfers between devices: 6.12 us -> 19.7 us  [padded_2(): lax.ppermute(lax.slice_in_dim(block, block.shape[dim] - width, None, axis...]
    ppermute x0 -> x7, waiting for transfers between devices: none -> 11.9 us  [launch_ports(): finding = lax.ppermute(finding, ax_name, frames)]
    ppermute x0 -> x7, starting transfers between devices: none -> 8.33 us  [launch_ports(): finding = lax.ppermute(finding, ax_name, frames)]
    sub x1, other arithmetic: 12.2 us -> 4.5 us  [attend(): expo = jnp.exp(scores - top)]
    dot_general x1, matrix products: 3.8 us -> 7.81 us  [attend(): jnp.einsum('phqk,pkhd->pqhd', weights, values, preferred_element_type=jnp...]
    ppermute x1, starting transfers between devices: 8.15 us -> 6.12 us  [padded_2(): lax.ppermute(lax.slice_in_dim(block, 0, width, axis=dim), axis, backward)]
  transfers between devices with their start and end apart: 2 -> 9, of which waited for: 2 -> 6; matrix products, arithmetic and copies ran while one was open for 1% -> 1% of each run, Pallas kernels for 0% -> 0%
where the time goes in v1:
time: 119 us
  waiting for transfers between devices  32.9 us (28%)
  matrix products  23.9 us (20%)
  blocking collectives  19.5 us (16%)
  starting transfers between devices  18.4 us (15%)
  local copies, waits for them, and re-layouts  17.3 us (15%)
  other arithmetic  6.44 us (5%)
    ppermute x1, waiting for transfers between devices, padded_2(): lax.ppermute(lax.slice_in_dim(block, block.shape[dim] - width, None, axis...  19.7 us
    all_to_all x1, blocking collectives, shards(): lax.all_to_all(attended_px, 'lead', split_axis=2, concat_axis=1, tiled=True)  19.5 us
    ppermute x7, waiting for transfers between devices, launch_ports(): finding = lax.ppermute(finding, ax_name, frames)  11.9 us
    ppermute x7, starting transfers between devices, launch_ports(): finding = lax.ppermute(finding, ax_name, frames)  8.33 us
    dot_general x1, matrix products, attend(): jnp.einsum('phqk,pkhd->pqhd', weights, values, preferred_element_type=jnp...  7.81 us
    dot_general x9, matrix products, shards(): jnp.dot(piece, conv_weight[a, b], preferred_element_type=jnp.float32)  6.44 us
    ppermute x1, starting transfers between devices, padded_2(): lax.ppermute(lax.slice_in_dim(block, 0, width, axis=dim), axis, backward)  6.12 us
    dot_general x1, matrix products, attend(): jnp.einsum('pqhd,pkhd->phqk', query, keys, preferred_element_type=jnp.flo...  5.02 us
  transfers between devices with their start and end apart: 9, of which 6 were waited for; matrix products, arithmetic and copies ran while one was open for 1% of the time, Pallas kernels for 0%

profile of v1, /device:TPU:6, one launch (start us, length us, event | category | flops | bytes accessed | tf_op | source)
XLA Modules:
  0.0 118.7 jit_solution(8214232237816704027)
XLA Ops:
  0.0 3.9 %collective-permute-start = (bf16[1,256,8,256]{3,2,1,0:T(8,128)(2,1)}, bf16[1,256,8,256]{3,2,1,0:T(8,128)(2,1)S(1)}, u32[]{:S(2)}, u32[]{:S(2)}) collective-permute-start(bf16[1,256,8,256]{3,2,1,0:T(8,128)(2,1)} %param.8), channel_id=1, source_target_pairs={{0,8},{8,16},{16,24},{24,32},{32,40},{40,48},{48,56},{56,64},{64,7... | collective-permute-start | bytes 3145736 | tf_op jit(solution)/shard_map/ppermute | solution.py:43
  4.0 6.1 %collective-permute-start.1 = (bf16[1,256,8,256]{3,2,1,0:T(8,128)(2,1)}, bf16[1,256,8,256]{3,2,1,0:T(8,128)(2,1)S(1)}, u32[]{:S(2)}, u32[]{:S(2)}) collective-permute-start(bf16[1,256,8,256]{3,2,1,0:T(8,128)(2,1)} %param.8), channel_id=1, source_target_pairs={{8,0},{16,8},{24,16},{32,24},{40,32},{48,40},{56,48},{64,56},{72,6... | collective-permute-start | bytes 3145736 | tf_op jit(solution)/shard_map/ppermute | solution.py:46
  10.1 1.7 %fusion.46 = f32[2048,256]{1,0:T(8,128)S(1)} fusion(bf16[1,256,8,256]{3,2,1,0:T(8,128)(2,1)} %param.8, bf16[3,3,256,256]{3,2,1,0:T(8,128)(2,1)} %param.9), kind=kOutput, calls=%fused_computation.61 | convolution fusion | flops 268435456 | bytes 3276800 | tf_op jit(solution)/shard_map/dot_general | solution.py:82
  11.8 19.7 %collective-permute-done = bf16[1,256,8,256]{3,2,1,0:T(8,128)(2,1)S(1)} collective-permute-done((bf16[1,256,8,256]{3,2,1,0:T(8,128)(2,1)}, bf16[1,256,8,256]{3,2,1,0:T(8,128)(2,1)S(1)}, u32[]{:S(2)}, u32[]{:S(2)}) %collective-permute-start) | collective-permute-done | bytes 1048608 | tf_op jit(solution)/shard_map/ppermute | solution.py:43
  36.7 1.7 %convert_reduce_fusion = (f32[2048]{0:T(1024)S(1)}, bf16[2048,256]{1,0:T(8,128)(2,1)S(1)}) fusion(f32[256]{0:T(256)S(1)} %copy-done.6, f32[2048,256]{1,0:T(8,128)S(1)} %fusion.39, f32[2048,256]{1,0:T(8,128)S(1)} %fusion.44, f32[2048,256]{1,0:T(8,128)S(1)} %fusion.40, bf16[3,3,256,256]{3,2,1,0:T(8,128)(2,1)S(1)} %copy-done.2, ...), kind=kOutput, calls=%fused_computation.17 | convolution fusion | flops 278919168 | bytes 19014656 | tf_op jit(solution)/shard_map/dot_general | solution.py:82
  40.2 1.7 %collective-permute-start.3 = (bf16[1,32,8,256]{3,2,1,0:T(8,128)(2,1)S(1)}, bf16[1,32,8,256]{3,2,1,0:T(8,128)(2,1)S(1)}, u32[]{:S(2)}, u32[]{:S(2)}) collective-permute-start(bf16[1,32,8,256]{3,2,1,0:T(8,128)(2,1)S(1)} %get-tuple-element.10), channel_id=1, source_target_pairs={{0,2},{1,3},{2,0},{3,1},{4,6},{5,7},{6,4},{7,5},{8,10},{9,11},{10,... | collective-permute-start | bytes 393224 | tf_op jit(solution)/shard_map/ppermute | solution.py:29
  42.0 3.2 %collective-permute-start.5 = (bf16[1,32,8,256]{3,2,1,0:T(8,128)(2,1)S(1)}, bf16[1,32,8,256]{3,2,1,0:T(8,128)(2,1)S(1)}, u32[]{:S(2)}, u32[]{:S(2)}) collective-permute-start(bf16[1,32,8,256]{3,2,1,0:T(8,128)(2,1)S(1)} %get-tuple-element.8), channel_id=1, source_target_pairs={{0,4},{1,5},{2,6},{3,7},{4,0},{5,1},{6,2},{7,3},{8,12},{9,13},{10,... | collective-permute-start | bytes 393224 | tf_op jit(solution)/shard_map/ppermute | solution.py:29
  45.3 3.0 %collective-permute-start.7 = (bf16[1,32,8,256]{3,2,1,0:T(8,128)(2,1)S(1)}, bf16[1,32,8,256]{3,2,1,0:T(8,128)(2,1)S(1)}, u32[]{:S(2)}, u32[]{:S(2)}) collective-permute-start(bf16[1,32,8,256]{3,2,1,0:T(8,128)(2,1)S(1)} %get-tuple-element.6), channel_id=1, source_target_pairs={{0,6},{1,7},{2,4},{3,5},{4,2},{5,3},{6,0},{7,1},{8,14},{9,15},{10,... | collective-permute-start | bytes 393224 | tf_op jit(solution)/shard_map/ppermute | solution.py:29
  48.5 6.2 %collective-permute-done.5 = bf16[1,32,8,256]{3,2,1,0:T(8,128)(2,1)S(1)} collective-permute-done((bf16[1,32,8,256]{3,2,1,0:T(8,128)(2,1)S(1)}, bf16[1,32,8,256]{3,2,1,0:T(8,128)(2,1)S(1)}, u32[]{:S(2)}, u32[]{:S(2)}) %collective-permute-start.5) | collective-permute-done | bytes 131104 | tf_op jit(solution)/shard_map/ppermute | solution.py:29
  54.8 1.8 %collective-permute-done.6 = bf16[1,32,8,256]{3,2,1,0:T(8,128)(2,1)S(1)} collective-permute-done((bf16[1,32,8,256]{3,2,1,0:T(8,128)(2,1)S(1)}, bf16[1,32,8,256]{3,2,1,0:T(8,128)(2,1)S(1)}, u32[]{:S(2)}, u32[]{:S(2)}) %collective-permute-start.6) | collective-permute-done | bytes 131104 | tf_op jit(solution)/shard_map/ppermute | solution.py:29
  56.6 1.8 %collective-permute-done.7 = bf16[1,32,8,256]{3,2,1,0:T(8,128)(2,1)S(1)} collective-permute-done((bf16[1,32,8,256]{3,2,1,0:T(8,128)(2,1)S(1)}, bf16[1,32,8,256]{3,2,1,0:T(8,128)(2,1)S(1)}, u32[]{:S(2)}, u32[]{:S(2)}) %collective-permute-start.7) | collective-permute-done | bytes 131104 | tf_op jit(solution)/shard_map/ppermute | solution.py:29
  58.4 2.0 %collective-permute-done.8 = bf16[1,32,8,256]{3,2,1,0:T(8,128)(2,1)S(1)} collective-permute-done((bf16[1,32,8,256]{3,2,1,0:T(8,128)(2,1)S(1)}, bf16[1,32,8,256]{3,2,1,0:T(8,128)(2,1)S(1)}, u32[]{:S(2)}, u32[]{:S(2)}) %collective-permute-start.8) | collective-permute-done | bytes 131104 | tf_op jit(solution)/shard_map/ppermute | solution.py:29
  60.4 1.4 %convolution_convert_fusion.1 = bf16[2048,256]{1,0:T(8,128)(2,1)} fusion(bf16[2048,256]{1,0:T(8,128)(2,1)S(1)} %bitcast.86, bf16[256,256]{1,0:T(8,128)(2,1)S(1)} %copy-done), kind=kOutput, calls=%fused_computation.26 | convolution fusion | flops 268959744 | bytes 2228224 | tf_op jit(solution)/shard_map/dot_general | solution.py:70
  61.8 1.5 %copy.23 = bf16[2048,256]{0,1:T(8,128)(2,1)S(1)} copy(bf16[2048,256]{1,0:T(8,128)(2,1)} %convolution_convert_fusion.1) | data formatting | bytes 2097152 | tf_op jit(solution)/shard_map/convert_element_type | solution.py:71
  63.3 3.2 %reshape_reshape.10 = bf16[32,64,8,32]{1,0,3,2:T(8,128)(2,1)} reshape(bf16[2048,256]{0,1:T(8,128)(2,1)S(1)} %copy.23) | data formatting | bytes 2097152 | tf_op jit(solution)/shard_map/reshape;reshape | solution.py:55
  67.9 1.5 %copy.24 = bf16[2048,256]{0,1:T(8,128)(2,1)S(1)} copy(bf16[2048,256]{1,0:T(8,128)(2,1)} %convolution_convert_fusion) | data formatting | bytes 2097152 | tf_op jit(solution)/shard_map/convert_element_type | solution.py:71
  69.4 3.2 %reshape_reshape.11 = bf16[32,64,8,32]{1,0,3,2:T(8,128)(2,1)} reshape(bf16[2048,256]{0,1:T(8,128)(2,1)S(1)} %copy.24) | data formatting | bytes 2097152 | tf_op jit(solution)/shard_map/reshape;reshape | solution.py:56
  72.6 5.0 %fusion.31 = f32[32,8,64,64]{2,3,1,0:T(8,128)S(1)} fusion(bf16[32,64,8,32]{1,0,3,2:T(8,128)(2,1)} %reshape_reshape.11, bf16[32,64,8,32]{1,0,3,2:T(8,128)(2,1)} %reshape_reshape.10), kind=kOutput, calls=%fused_computation.42 | convolution fusion | flops 67108864 | bytes 6291456 | tf_op jit(solution)/shard_map/pqhd,pkhd->phqk/dot_general | solution.py:58
  77.7 4.5 %fusion.69 = (f32[32,8,64]{2,1,0:T(8,128)S(1)}, f32[32,8,64,64]{2,3,1,0:T(8,128)}) fusion(f32[32,8,64,64]{2,3,1,0:T(8,128)S(1)} %fusion.31), kind=kOutput, calls=%fused_computation.102 | output fusion | flops 4194367 | bytes 8454144 | tf_op jit(solution)/shard_map/sub | solution.py:62
  83.3 3.1 %reshape_reshape.9 = bf16[32,64,8,32]{1,0,3,2:T(8,128)(2,1)} reshape(bf16[2048,256]{0,1:T(8,128)(2,1)S(1)} %copy.22) | data formatting | bytes 2097152 | tf_op jit(solution)/shard_map/reshape;reshape | solution.py:57
  86.4 7.8 %fusion.34 = bf16[32,8,32,64]{3,2,1,0:T(8,128)(2,1)} fusion(f32[32,8,64,64]{2,3,1,0:T(8,128)} %get-tuple-element.16, f32[32,8,64]{2,1,0:T(8,128)S(1)} %get-tuple-element.15, bf16[32,64,8,32]{1,0,3,2:T(8,128)(2,1)} %reshape_reshape.9), kind=kOutput, calls=%fused_computation.45 | convolution fusion | flops 69730304 | bytes 6356992 | tf_op jit(solution)/shard_map/phqk,pkhd->pqhd/dot_general | solution.py:64
  94.2 2.7 %copy.29 = bf16[1,32,64,256]{3,1,0,2:T(8,128)(2,1)S(1)} copy(bf16[1,32,64,256]{2,3,1,0:T(8,128)(2,1)} %bitcast.91) | data formatting | bytes 2097152 | tf_op jit(solution)/shard_map/reshape | solution.py:65
  96.9 19.5 %all_to_all.15 = bf16[1,32,64,256]{3,1,0,2:T(8,128)(2,1)S(1)} all-to-all(bf16[1,32,64,256]{3,1,0,2:T(8,128)(2,1)S(1)} %copy.29), channel_id=1, replica_groups=mesh['lat'=32,'lead'=8] {'lead'}, dimensions={2} | all-to-all | bytes 2097152 | tf_op jit(solution)/shard_map/all_to_all | solution.py:91
  117.3 1.4 %fusion.37 = bf16[1,256,8,256]{3,2,1,0:T(8,128)(2,1)} fusion(bf16[2048,256]{1,0:T(8,128)(2,1)S(1)} %bitcast.89, bf16[256,256]{1,0:T(8,128)(2,1)S(1)} %copy-done.5, bf16[2048,256]{1,0:T(8,128)(2,1)S(1)} %get-tuple-element.14), kind=kOutput, calls=%fused_computation.46 | convolution fusion | flops 270008320 | bytes 3276800 | tf_op jit(solution)/shard_map/dot_general | solution.py:92
  (50 shorter events, 10.7 us)
Async XLA Ops:
  0.0 60.4 %copy-start = (bf16[256,256]{1,0:T(8,128)(2,1)S(1)}, bf16[256,256]{1,0:T(8,128)(2,1)}, u32[]{:S(2)}) copy-start(bf16[256,256]{1,0:T(8,128)(2,1)} %param.12) | copy-start | bytes 393220
  0.0 32.8 %copy-start.1 = (bf16[1,256,8,256]{3,2,1,0:T(8,128)(2,1)S(1)}, bf16[1,256,8,256]{3,2,1,0:T(8,128)(2,1)}, u32[]{:S(2)}) copy-start(bf16[1,256,8,256]{3,2,1,0:T(8,128)(2,1)} %param.8) | copy-start | bytes 3145732
  0.0 31.5 %collective-permute-start = (bf16[1,256,8,256]{3,2,1,0:T(8,128)(2,1)}, bf16[1,256,8,256]{3,2,1,0:T(8,128)(2,1)S(1)}, u32[]{:S(2)}, u32[]{:S(2)}) collective-permute-start(bf16[1,256,8,256]{3,2,1,0:T(8,128)(2,1)} %param.8), channel_id=1, source_target_pairs={{0,8},{8,16},{16,24},{24,32},{32,40},{40,48},{48,56},{56,64},{64,7... | collective-permute-start | bytes 3145736 | tf_op jit(solution)/shard_map/ppermute | solution.py:43
  4.0 28.8 %collective-permute-start.1 = (bf16[1,256,8,256]{3,2,1,0:T(8,128)(2,1)}, bf16[1,256,8,256]{3,2,1,0:T(8,128)(2,1)S(1)}, u32[]{:S(2)}, u32[]{:S(2)}) collective-permute-start(bf16[1,256,8,256]{3,2,1,0:T(8,128)(2,1)} %param.8), channel_id=1, source_target_pairs={{8,0},{16,8},{24,16},{32,24},{40,32},{48,40},{56,48},{64,56},{72,6... | collective-permute-start | bytes 3145736 | tf_op jit(solution)/shard_map/ppermute | solution.py:46
  11.8 21.6 %copy-start.2 = (bf16[3,3,256,256]{3,2,1,0:T(8,128)(2,1)S(1)}, bf16[3,3,256,256]{3,2,1,0:T(8,128)(2,1)}, u32[]{:S(2)}) copy-start(bf16[3,3,256,256]{3,2,1,0:T(8,128)(2,1)} %param.9) | copy-start | bytes 3538948
  36.0 0.7 copy-start.6
  36.7 2.4 %copy-start.7 = (f32[256]{0:T(256)S(1)}, f32[256]{0:T(256)}, u32[]{:S(2)}) copy-start(f32[256]{0:T(256)} %param.11) | copy-start | bytes 3076
  40.1 5.2 %collective-permute-start.2 = (bf16[1,32,8,256]{3,2,1,0:T(8,128)(2,1)S(1)}, bf16[1,32,8,256]{3,2,1,0:T(8,128)(2,1)S(1)}, u32[]{:S(2)}, u32[]{:S(2)}) collective-permute-start(bf16[1,32,8,256]{3,2,1,0:T(8,128)(2,1)S(1)} %get-tuple-element.11), channel_id=1, source_target_pairs={{0,1},{1,0},{2,3},{3,2},{4,5},{5,4},{6,7},{7,6},{8,9},{9,8},{10,11... | collective-permute-start | bytes 393224 | tf_op jit(solution)/shard_map/ppermute | solution.py:29
  40.2 8.1 %collective-permute-start.3 = (bf16[1,32,8,256]{3,2,1,0:T(8,128)(2,1)S(1)}, bf16[1,32,8,256]{3,2,1,0:T(8,128)(2,1)S(1)}, u32[]{:S(2)}, u32[]{:S(2)}) collective-permute-start(bf16[1,32,8,256]{3,2,1,0:T(8,128)(2,1)S(1)} %get-tuple-element.10), channel_id=1, source_target_pairs={{0,2},{1,3},{2,0},{3,1},{4,6},{5,7},{6,4},{7,5},{8,10},{9,11},{10,... | collective-permute-start | bytes 393224 | tf_op jit(solution)/shard_map/ppermute | solution.py:29
  41.8 6.6 %collective-permute-start.4 = (bf16[1,32,8,256]{3,2,1,0:T(8,128)(2,1)S(1)}, bf16[1,32,8,256]{3,2,1,0:T(8,128)(2,1)S(1)}, u32[]{:S(2)}, u32[]{:S(2)}) collective-permute-start(bf16[1,32,8,256]{3,2,1,0:T(8,128)(2,1)S(1)} %get-tuple-element.9), channel_id=1, source_target_pairs={{0,3},{1,2},{2,1},{3,0},{4,7},{5,6},{6,5},{7,4},{8,11},{9,10},{10,... | collective-permute-start | bytes 393224 | tf_op jit(solution)/shard_map/ppermute | solution.py:29
  42.0 12.7 %collective-permute-start.5 = (bf16[1,32,8,256]{3,2,1,0:T(8,128)(2,1)S(1)}, bf16[1,32,8,256]{3,2,1,0:T(8,128)(2,1)S(1)}, u32[]{:S(2)}, u32[]{:S(2)}) collective-permute-start(bf16[1,32,8,256]{3,2,1,0:T(8,128)(2,1)S(1)} %get-tuple-element.8), channel_id=1, source_target_pairs={{0,4},{1,5},{2,6},{3,7},{4,0},{5,1},{6,2},{7,3},{8,12},{9,13},{10,... | collective-permute-start | bytes 393224 | tf_op jit(solution)/shard_map/ppermute | solution.py:29
  45.3 11.3 %collective-permute-start.6 = (bf16[1,32,8,256]{3,2,1,0:T(8,128)(2,1)S(1)}, bf16[1,32,8,256]{3,2,1,0:T(8,128)(2,1)S(1)}, u32[]{:S(2)}, u32[]{:S(2)}) collective-permute-start(bf16[1,32,8,256]{3,2,1,0:T(8,128)(2,1)S(1)} %get-tuple-element.7), channel_id=1, source_target_pairs={{0,5},{1,4},{2,7},{3,6},{4,1},{5,0},{6,3},{7,2},{8,13},{9,12},{10,... | collective-permute-start | bytes 393224 | tf_op jit(solution)/shard_map/ppermute | solution.py:29
  45.3 13.1 %collective-permute-start.7 = (bf16[1,32,8,256]{3,2,1,0:T(8,128)(2,1)S(1)}, bf16[1,32,8,256]{3,2,1,0:T(8,128)(2,1)S(1)}, u32[]{:S(2)}, u32[]{:S(2)}) collective-permute-start(bf16[1,32,8,256]{3,2,1,0:T(8,128)(2,1)S(1)} %get-tuple-element.6), channel_id=1, source_target_pairs={{0,6},{1,7},{2,4},{3,5},{4,2},{5,3},{6,0},{7,1},{8,14},{9,15},{10,... | collective-permute-start | bytes 393224 | tf_op jit(solution)/shard_map/ppermute | solution.py:29
  48.3 12.1 %collective-permute-start.8 = (bf16[1,32,8,256]{3,2,1,0:T(8,128)(2,1)S(1)}, bf16[1,32,8,256]{3,2,1,0:T(8,128)(2,1)S(1)}, u32[]{:S(2)}, u32[]{:S(2)}) collective-permute-start(bf16[1,32,8,256]{3,2,1,0:T(8,128)(2,1)S(1)} %get-tuple-element.5), channel_id=1, source_target_pairs={{0,7},{1,6},{2,5},{3,4},{4,3},{5,2},{6,1},{7,0},{8,15},{9,14},{10,... | collective-permute-start | bytes 393224 | tf_op jit(solution)/shard_map/ppermute | solution.py:29
  63.3 3.2 %copy-start.3 = (bf16[256,256]{1,0:T(8,128)(2,1)S(1)}, bf16[256,256]{1,0:T(8,128)(2,1)}, u32[]{:S(2)}) copy-start(bf16[256,256]{1,0:T(8,128)(2,1)} %param.13) | copy-start | bytes 393220
  77.6 4.5 %copy-start.4 = (bf16[256,256]{1,0:T(8,128)(2,1)S(1)}, bf16[256,256]{1,0:T(8,128)(2,1)}, u32[]{:S(2)}) copy-start(bf16[256,256]{1,0:T(8,128)(2,1)} %param.14) | copy-start | bytes 393220
  116.4 0.9 copy-start.5
